TPU v7x, 32 devices: a whole 2x2x4 slice. The times are simulated.
32 devices in a mesh: expert: 16 (over z, y, x), loop: 2 (over core).
Axes of the slice: x: 2, y: 2, z: 4, core: 2. Of those that a mesh axis runs over, the one named last changes fastest.
Arguments:
- tokens: bfloat16 [2048, 7168], P('expert', 'loop'), may hold values from -6 to 6
- expert_ids: int32 [2048, 8], P('expert'), may hold values from 0 to 255, all different within a row; in each aligned block of 128 rows (0 to 127, 128 to 255, ...) at most 8 rows name the same one
- route_weights: float32 [2048, 8], P('expert'), may hold values from 0.1 to 1
- up_proj: bfloat16 [16, 7168, 1024], P('expert', None, 'loop'), may hold values from -0.0625 to 0.0625
- down_proj: bfloat16 [16, 1024, 7168], P('expert', None, 'loop'), may hold values from -0.1875 to 0.1875
Outputs:
- combined: bfloat16 [2048, 7168], P('expert', 'loop')
Inputs may be any that keep to these rules, and one draw needn't show every extreme that they name: `expert_ids`: each row names 8 different experts. Among the 128 rows held by one device along `expert`, no expert is chosen by more than 8 rows, a bound that some block reaches.
All inputs are finite; a program needn't handle non-finite values.
Results may differ from a plain program's by a relative error of at most 0.0058.
Values may be sent and summed in bfloat16 or wider, within the bound.
No kernel may reach another device: no remote copies, remote signals or barrier semaphores. Data moves between devices by JAX's collectives and lax.ppermute only.
A program may use at most 64 MiB of HBM per device.

v0:
```python
import jax
import jax.numpy as jnp
from jax import lax
from jax.sharding import PartitionSpec as P


def slot_tables(expert_ids, route_weights, flight, capacity):
    tok_count = expert_ids.shape[0]
    experts = jnp.arange(flight, dtype=jnp.int32)
    matches = expert_ids[:, :, None] == experts[None, None, :]
    chosen = jnp.any(matches, axis=1)
    weight = jnp.sum(jnp.where(matches, route_weights[:, :, None], 0.0), axis=1)
    ranking = jnp.cumsum(chosen.astype(jnp.int32), axis=0) - 1
    places = jnp.arange(capacity, dtype=jnp.int32)
    picked = chosen[:, :, None] & (ranking[:, :, None] == places[None, None, :])
    tok_index = jnp.arange(tok_count, dtype=jnp.int32)
    slot_token = jnp.sum(jnp.where(picked, tok_index[:, None, None], 0), axis=0).reshape(
        flight * capacity
    )
    slot_weight = jnp.sum(jnp.where(picked, weight[:, :, None], 0.0), axis=0).reshape(
        flight * capacity
    )
    slot_live = jnp.any(picked, axis=0).reshape(flight * capacity)
    return (slot_token, slot_weight, slot_live)


def on_device(tokens, expert_ids, route_weights, up_proj, down_proj):
    tok_rows = tokens.shape[0]
    capacity = tok_rows // 16
    owners = lax.axis_size("expert")
    per_owner = up_proj.shape[0]
    flight = owners * per_owner
    slot_count = owners * capacity
    slot_token, slot_weight, slot_live = slot_tables(expert_ids, route_weights, flight, capacity)
    live_mask = slot_live.astype(jnp.bfloat16)[:, None]
    features = lax.all_gather(tokens, "loop", axis=1, tiled=True)
    full_width = features.shape[1]
    outgoing = (jnp.take(features, slot_token, axis=0) * live_mask).reshape(
        owners, per_owner * capacity, full_width
    )
    arrived = lax.all_to_all(outgoing, "expert", split_axis=0, concat_axis=0, tiled=True)
    slot_rows = (
        arrived.reshape(owners, per_owner, capacity, full_width)
        .transpose(1, 0, 2, 3)
        .reshape(per_owner, slot_count, full_width)
    )
    up_sums = jnp.einsum("esd,edh->esh", slot_rows, up_proj, preferred_element_type=jnp.float32)
    hidden = jax.nn.silu(up_sums).astype(jnp.bfloat16)
    out_width = down_proj.shape[2]
    out_rows = jnp.einsum(
        "esh,ehd->esd",
        lax.all_gather(hidden, "loop", axis=2, tiled=True),
        down_proj,
        preferred_element_type=jnp.float32,
    ).astype(jnp.bfloat16)
    homeward = (
        out_rows.reshape(per_owner, owners, capacity, out_width)
        .transpose(1, 0, 2, 3)
        .reshape(owners, per_owner * capacity, out_width)
    )
    returned = lax.all_to_all(homeward, "expert", split_axis=0, concat_axis=0, tiled=True).reshape(
        flight * capacity, out_width
    )
    scaled = slot_weight[:, None] * returned.astype(jnp.float32)
    combined = jax.ops.segment_sum(scaled, slot_token, num_segments=tok_rows)
    return combined.astype(jnp.bfloat16)


def solution(mesh):
    return jax.shard_map(
        on_device,
        mesh=mesh,
        in_specs=(
            P("expert", "loop"),
            P("expert", None),
            P("expert", None),
            P("expert", None, "loop"),
            P("expert", None, "loop"),
        ),
        out_specs=P("expert", "loop"),
        check_vma=False,
    )
```

profile of v0, /device:TPU:0, one launch (start us, length us, event | category | flops | bytes accessed | tf_op | source)
XLA Modules:
  0.0 124.3 jit_solution(4287521138012820241)
XLA Ops:
  6.5 0.7 all-gather.3.cloned.1.call-update
  7.3 0.7 fusion.20
  8.0 0.1 copy.10
  8.1 0.2 reduce_window_sum.11
  8.3 0.1 copy.11
  8.3 0.4 select_reduce_fusion.2
  8.7 0.1 broadcast_in_dim_reshape.4
  8.8 0.4 fusion.22
  9.2 12.6 %all-gather.3.cloned.1.call-done = bf16[128,7168]{1,0:T(8,128)(2,1)} async-done(((bf16[128,3584]{1,0:T(8,128)(2,1)}), bf16[128,7168]{1,0:T(8,128)(2,1)}) %all-gather.3.cloned.1.call-update) | async-done | bytes 1835024 | tf_op jit(solution)/shard_map/all_gather | solution.py:36
  21.8 5.1 %gather_fusion = bf16[128,7168]{1,0:T(8,128)(2,1)S(1)} fusion(bf16[128,7168]{1,0:T(8,128)(2,1)} %all-gather.3.cloned.1.call-done, s32[1024]{0:T(1024)S(1)} %pad_clamp_fusion), kind=kCustom, calls=%fused_computation | custom fusion | bytes 3670528 | tf_op jit(solution)/shard_map/jit(_take)/gather | solution.py:38
  26.9 0.2 fusion.12
  27.2 0.0 slice-start
  27.2 51.1 %all_to_all.10 = bf16[16,8,7168]{2,1,0:T(8,128)(2,1)S(1)} all-to-all(bf16[16,8,7168]{2,1,0:T(8,128)(2,1)S(1)} %fusion.12), channel_id=1, replica_groups=mesh['expert'=16,'loop'=2] {'expert'}, dimensions={0} | all-to-all | bytes 3670016 | tf_op jit(solution)/shard_map/all_to_all | solution.py:41
  78.3 4.4 %multiply_convert_fusion = bf16[128,512]{1,0:T(8,128)(2,1)S(1)} fusion(bf16[1,7168,512]{2,1,0:T(8,128)(2,1)} %param.8, bf16[16,8,7168]{2,1,0:T(8,128)(2,1)S(1)} %all_to_all.10), kind=kOutput, calls=%fused_computation.16 | convolution fusion | flops 939851776 | bytes 9306112 | tf_op jit(solution)/shard_map/esd,edh->esh/dot_general | solution.py:47
  82.7 2.0 %all-gather = bf16[128,1024]{1,0:T(8,128)(2,1)S(1)} all-gather(bf16[128,512]{1,0:T(8,128)(2,1)S(1)} %multiply_convert_fusion), channel_id=2, replica_groups=mesh['expert'=16,'loop'=2] {'loop'}, dimensions={1}, use_global_device_ids=true | all-gather | bytes 393216 | tf_op jit(solution)/shard_map/all_gather | solution.py:52
  84.7 0.0 slice-done
  84.7 2.1 %fusion.7 = bf16[16,8,3584]{2,1,0:T(8,128)(2,1)} fusion(bf16[128,1024]{1,0:T(8,128)(2,1)S(1)} %all-gather, bf16[1,1024,3584]{2,1,0:T(8,128)(2,1)S(1)} %bitcast.33), kind=kOutput, calls=%fused_computation.7 | convolution fusion | flops 939982848 | bytes 8519680 | tf_op jit(solution)/shard_map/esh,ehd->esd/dot_general | solution.py:50
  86.7 3.8 %all-to-all-start.1 = ((bf16[16,8,3584]{2,1,0:T(8,128)(2,1)}), bf16[16,8,3584]{2,1,0:T(8,128)(2,1)S(1)}, u32[]{:S(2)}, u32[]{:S(2)}) async-start(bf16[16,8,3584]{2,1,0:T(8,128)(2,1)} %fusion.7), calls=%async_computation.1 | async-start | bytes 1835008 | tf_op jit(solution)/shard_map/all_to_all | solution.py:61
  90.5 0.1 reshape.106
  90.6 0.1 select_reduce_fusion
  90.7 0.1 mul.24
  90.8 22.0 %all-to-all-done.1 = bf16[16,8,3584]{2,1,0:T(8,128)(2,1)S(1)} async-done(((bf16[16,8,3584]{2,1,0:T(8,128)(2,1)}), bf16[16,8,3584]{2,1,0:T(8,128)(2,1)S(1)}, u32[]{:S(2)}, u32[]{:S(2)}) %all-to-all-start.1) | async-done | bytes 917536 | tf_op jit(solution)/shard_map/all_to_all | solution.py:61
  112.8 3.6 %scatter_custom_fusion = f32[128,3584]{1,0:T(8,128)S(1)} fusion(s32[128]{0:T(128)S(1)} %reshape.106, bf16[16,8,3584]{2,1,0:T(8,128)(2,1)S(1)} %all-to-all-done.1, f32[128]{0:T(128)S(1)} %mul.24, f32[]{:T(128)} %constant.11.clone.1), kind=kCustom, calls=%fused_computation.9 | custom fusion | flops 1376256 | bytes 2753028 | tf_op jit(solution)/shard_map/scatter-add | solution.py:65
  116.4 1.0 convert_element_type.40
  (15 shorter events, 0.1 us)
Async XLA Ops:
  6.5 15.3 %all-gather.3.cloned.1.call-start = ((), (), s32[]{:S(2)}) async-start(), calls=%async_computation.2 | async-start | bytes 2752512 | tf_op jit(solution)/shard_map/all_gather | solution.py:36
  27.2 57.5 %slice-start = ((s8[7340032]{0:T(1024)(128)(4,1)}), s8[4194304]{0:T(1024)(128)(4,1)S(1)}, s32[]{:S(2)}) async-start(s8[7340032]{0:T(1024)(128)(4,1)} %bitcast.32), calls=%async_computation.3 | async-start | bytes 8388608
  78.3 6.4 %slice-start.1 = ((s8[7340032]{0:T(1024)(128)(4,1)}), s8[3145728]{0:T(1024)(128)(4,1)S(1)}, s32[]{:S(2)}) async-start(s8[7340032]{0:T(1024)(128)(4,1)} %bitcast.32), calls=%async_computation.4 | async-start | bytes 6291456
  86.7 3.9 %copy-start = (s32[128,8]{0,1:T(8,128)S(1)}, s32[128,8]{0,1:T(8,128)}, u32[]{:S(2)}) copy-start(s32[128,8]{0,1:T(8,128)} %param.6) | copy-start | bytes 12292
  86.7 3.9 %copy-start.1 = (f32[128,8]{0,1:T(8,128)S(1)}, f32[128,8]{0,1:T(8,128)}, u32[]{:S(2)}) copy-start(f32[128,8]{0,1:T(8,128)} %param.7) | copy-start | bytes 12292
  86.7 26.1 %all-to-all-start.1 = ((bf16[16,8,3584]{2,1,0:T(8,128)(2,1)}), bf16[16,8,3584]{2,1,0:T(8,128)(2,1)S(1)}, u32[]{:S(2)}, u32[]{:S(2)}) async-start(bf16[16,8,3584]{2,1,0:T(8,128)(2,1)} %fusion.7), calls=%async_computation.1 | async-start | bytes 1835008 | tf_op jit(solution)/shard_map/all_to_all | solution.py:61
Sparse Core Ops, SparseCore 0:
  8.9 12.8 all-gather.2
where the time goes:
time: 125 us; the launch traced here: 124 us
  blocking collectives  53.1 us (42%)
  waiting for transfers between devices  35.3 us (28%)
  between operations  13.5 us (11%)
  other arithmetic  6.58 us (5%)
  matrix products  6.47 us (5%)
  local copies, waits for them, and re-layouts  5.53 us (4%)
  starting transfers between devices  3.77 us (3%)
    all_to_all x1, blocking collectives, on_device(): lax.all_to_all(outgoing, 'expert', split_axis=0, concat_axis=0, tiled=True)  51.1 us
    all_to_all x1, waiting for transfers between devices, on_device(): lax.all_to_all(homeward, 'expert', split_axis=0, concat_axis=0, tiled=True)  22 us
    all_gather x1, waiting for transfers between devices, on_device(): features = lax.all_gather(tokens, 'loop', axis=1, tiled=True)  12.6 us
    gather x1, local copies, waits for them, and re-layouts, on_device(): jnp.take(features, slot_token, axis=0) * live_mask  5.1 us
    dot_general x1, matrix products, on_device(): jnp.einsum('esd,edh->esh', slot_rows, up_proj, preferred_element_type=jnp...  4.4 us
    all_to_all x1, starting transfers between devices, on_device(): lax.all_to_all(homeward, 'expert', split_axis=0, concat_axis=0, tiled=True)  3.77 us
    scatter-add x1, other arithmetic, on_device(): combined = jax.ops.segment_sum(scaled, slot_token, num_segments=tok_rows)  3.58 us
  transfers between devices with their start and end apart: 2, of which 2 were waited for; matrix products, arithmetic and copies ran while one was open for 2% of the time, Pallas kernels for 0%

commit v1 on v0

--- a/solution.py
+++ b/solution.py
@@ -2,6 +2,17 @@
 import jax.numpy as jnp
 from jax import lax
 from jax.sharding import PartitionSpec as P
+
+
+def cut_along(x, dim, size):
+    before, after = (x.shape[:dim], x.shape[dim + 1 :])
+    return jnp.moveaxis(x.reshape(*before, size, -1, *after), dim, 0)
+
+
+def in_order(blocks, dim):
+    blocks = jnp.moveaxis(blocks, 0, dim)
+    shape = blocks.shape
+    return blocks.reshape(*shape[:dim], shape[dim] * shape[dim + 1], *shape[dim + 2 :])
 
 
 def slot_tables(expert_ids, route_weights, flight, capacity):
@@ -38,7 +49,15 @@
     outgoing = (jnp.take(features, slot_token, axis=0) * live_mask).reshape(
         owners, per_owner * capacity, full_width
     )
-    arrived = lax.all_to_all(outgoing, "expert", split_axis=0, concat_axis=0, tiled=True)
+    count, index = (lax.axis_size("expert"), lax.axis_index("expert"))
+    tiles = cut_along(outgoing, 0, count)
+    filled = tiles
+    for hop in range(1, count):
+        target, source = ((index + hop) % count, (index - hop) % count)
+        sent = lax.dynamic_index_in_dim(tiles, target, 0)
+        other = lax.ppermute(sent, "expert", [(i, (i + hop) % count) for i in range(count)])
+        filled = lax.dynamic_update_slice_in_dim(filled, other, source, axis=0)
+    arrived = in_order(filled, 0)
     slot_rows = (
         arrived.reshape(owners, per_owner, capacity, full_width)
         .transpose(1, 0, 2, 3)

time: 125 us -> 166 us (1.33)
  waiting for transfers between devices: 35.3 us -> 104 us
  blocking collectives: 53.1 us -> 1.99 us
  starting transfers between devices: 3.77 us -> 23.7 us
  local copies, waits for them, and re-layouts: 5.53 us -> 7.8 us
    ppermute x0 -> x15, waiting for transfers between devices: none -> 68.4 us  [on_device(): lax.ppermute(sent, 'expert', [(i, (i + hop) % count) for i in range(count)])]
    all_to_all x1 -> x0, blocking collectives: 51.1 us -> none  [on_device(): lax.all_to_all(outgoing, 'expert', split_axis=0, concat_axis=0, tiled=True)]
    ppermute x0 -> x15, starting transfers between devices: none -> 14.4 us  [on_device(): lax.ppermute(sent, 'expert', [(i, (i + hop) % count) for i in range(count)])]
    all_to_all x1, starting transfers between devices: 3.77 us -> 9.26 us  [on_device(): lax.all_to_all(homeward, 'expert', split_axis=0, concat_axis=0, tiled=True)]
  transfers between devices with their start and end apart: 2 -> 17, of which waited for: 2 -> 13; matrix products, arithmetic and copies ran while one was open for 2% -> 1% of each run, Pallas kernels for 0% -> 0%
where the time goes in v1:
time: 166 us; the launch traced here: 165 us
  waiting for transfers between devices  104 us (63%)
  starting transfers between devices  23.7 us (14%)
  between operations  13.7 us (8%)
  other arithmetic  8.08 us (5%)
  local copies, waits for them, and re-layouts  7.8 us (5%)
  matrix products  6.47 us (4%)
  blocking collectives  1.99 us (1%)
    ppermute x15, waiting for transfers between devices, on_device(): lax.ppermute(sent, 'expert', [(i, (i + hop) % count) for i in range(count)])  68.4 us
    all_to_all x1, waiting for transfers between devices, on_device(): lax.all_to_all(homeward, 'expert', split_axis=0, concat_axis=0, tiled=True)  22 us
    ppermute x15, starting transfers between devices, on_device(): lax.ppermute(sent, 'expert', [(i, (i + hop) % count) for i in range(count)])  14.4 us
    all_gather x1, waiting for transfers between devices, on_device(): features = lax.all_gather(tokens, 'loop', axis=1, tiled=True)  12.6 us
    all_to_all x1, starting transfers between devices, on_device(): lax.all_to_all(homeward, 'expert', split_axis=0, concat_axis=0, tiled=True)  9.26 us
    gather x1, local copies, waits for them, and re-layouts, on_device(): jnp.take(features, slot_token, axis=0) * live_mask  6.33 us
    dot_general x1, matrix products, on_device(): jnp.einsum('esd,edh->esh', slot_rows, up_proj, preferred_element_type=jnp...  4.41 us
    scatter-add x1, other arithmetic, on_device(): combined = jax.ops.segment_sum(scaled, slot_token, num_segments=tok_rows)  3.58 us
  transfers between devices with their start and end apart: 17, of which 13 were waited for; matrix products, arithmetic and copies ran while one was open for 1% of the time, Pallas kernels for 0%

profile of v1, /device:TPU:0, one launch (start us, length us, event | category | flops | bytes accessed | tf_op | source)
XLA Modules:
  0.0 165.4 jit_solution(5427250087384471375)
XLA Ops:
  9.2 12.6 %all-gather.3.cloned.1.call-done = bf16[128,7168]{1,0:T(8,128)(2,1)} async-done(((bf16[128,3584]{1,0:T(8,128)(2,1)}), bf16[128,7168]{1,0:T(8,128)(2,1)}) %all-gather.3.cloned.1.call-update) | async-done | bytes 1835024 | tf_op jit(solution)/shard_map/all_gather | solution.py:47
  21.8 6.3 %gather_fusion = bf16[128,7168]{1,0:T(8,128)(2,1)} fusion(bf16[128,7168]{1,0:T(8,128)(2,1)} %all-gather.3.cloned.1.call-done, s32[1024]{0:T(1024)S(1)} %pad_clamp_fusion), kind=kCustom, calls=%fused_computation | custom fusion | bytes 3670528 | tf_op jit(solution)/shard_map/jit(_take)/gather | solution.py:49
  28.2 1.7 %fusion.12 = bf16[16,1,8,7168]{3,2,0,1:T(8,128)(2,1)S(1)} fusion(bf16[128,7168]{1,0:T(8,128)(2,1)} %gather_fusion, pred[16,8]{1,0:T(8,128)(4,1)S(1)} %compare_and_fusion, bf16[16,8]{1,0:T(8,128)(2,1)S(1)} %convert_element_type.34), kind=kLoop, calls=%fused_computation.12 | loop fusion | flops 1835008 | bytes 3670400 | tf_op jit(solution)/shard_map/mul | solution.py:49
  29.9 1.8 %collective-permute-start = (bf16[1,1,8,7168]{3,2,0,1:T(8,128)(2,1)S(1)}, bf16[1,1,8,7168]{3,2,0,1:T(8,128)(2,1)S(1)}, u32[]{:S(2)}, u32[]{:S(2)}) collective-permute-start(bf16[1,1,8,7168]{3,2,0,1:T(8,128)(2,1)S(1)} %constant_dynamic-slice_fusion.14), channel_id=1, source_target_pairs={{0,2},{2,4},{4,6},{6,8},{8,10},{10,12},{12,14},{14,16},{16,18},{18... | collective-permute-start | bytes 344072 | tf_op jit(solution)/shard_map/ppermute | solution.py:58
  31.7 7.3 %collective-permute-done = bf16[1,1,8,7168]{3,2,0,1:T(8,128)(2,1)S(1)} collective-permute-done((bf16[1,1,8,7168]{3,2,0,1:T(8,128)(2,1)S(1)}, bf16[1,1,8,7168]{3,2,0,1:T(8,128)(2,1)S(1)}, u32[]{:S(2)}, u32[]{:S(2)}) %collective-permute-start) | collective-permute-done | bytes 114720 | tf_op jit(solution)/shard_map/ppermute | solution.py:58
  39.8 2.2 %collective-permute-start.14 = (bf16[1,1,8,7168]{3,2,0,1:T(8,128)(2,1)S(1)}, bf16[1,1,8,7168]{3,2,0,1:T(8,128)(2,1)S(1)}, u32[]{:S(2)}, u32[]{:S(2)}) collective-permute-start(bf16[1,1,8,7168]{3,2,0,1:T(8,128)(2,1)S(1)} %get-tuple-element.5), channel_id=1, source_target_pairs={{0,30},{2,0},{4,2},{6,4},{8,6},{10,8},{12,10},{14,12},{16,14},{18,... | collective-permute-start | bytes 344072 | tf_op jit(solution)/shard_map/ppermute | solution.py:58
  42.1 2.5 %collective-permute-start.13 = (bf16[1,1,8,7168]{3,2,0,1:T(8,128)(2,1)S(1)}, bf16[1,1,8,7168]{3,2,0,1:T(8,128)(2,1)S(1)}, u32[]{:S(2)}, u32[]{:S(2)}) collective-permute-start(bf16[1,1,8,7168]{3,2,0,1:T(8,128)(2,1)S(1)} %get-tuple-element.6), channel_id=1, source_target_pairs={{0,28},{2,30},{4,0},{6,2},{8,4},{10,6},{12,8},{14,10},{16,12},{18,... | collective-permute-start | bytes 344072 | tf_op jit(solution)/shard_map/ppermute | solution.py:58
  46.5 2.6 %collective-permute-done.1 = bf16[1,1,8,7168]{3,2,0,1:T(8,128)(2,1)S(1)} collective-permute-done((bf16[1,1,8,7168]{3,2,0,1:T(8,128)(2,1)S(1)}, bf16[1,1,8,7168]{3,2,0,1:T(8,128)(2,1)S(1)}, u32[]{:S(2)}, u32[]{:S(2)}) %collective-permute-start.1) | collective-permute-done | bytes 114720 | tf_op jit(solution)/shard_map/ppermute | solution.py:58
  49.1 7.5 %collective-permute-done.2 = bf16[1,1,8,7168]{3,2,0,1:T(8,128)(2,1)S(1)} collective-permute-done((bf16[1,1,8,7168]{3,2,0,1:T(8,128)(2,1)S(1)}, bf16[1,1,8,7168]{3,2,0,1:T(8,128)(2,1)S(1)}, u32[]{:S(2)}, u32[]{:S(2)}) %collective-permute-start.2) | collective-permute-done | bytes 114720 | tf_op jit(solution)/shard_map/ppermute | solution.py:58
  57.7 5.6 %collective-permute-done.3 = bf16[1,1,8,7168]{3,2,0,1:T(8,128)(2,1)S(1)} collective-permute-done((bf16[1,1,8,7168]{3,2,0,1:T(8,128)(2,1)}, bf16[1,1,8,7168]{3,2,0,1:T(8,128)(2,1)S(1)}, u32[]{:S(2)}, u32[]{:S(2)}) %collective-permute-start.3) | collective-permute-done | bytes 114720 | tf_op jit(solution)/shard_map/ppermute | solution.py:58
  63.4 10.2 %collective-permute-done.4 = bf16[1,1,8,7168]{3,2,0,1:T(8,128)(2,1)S(1)} collective-permute-done((bf16[1,1,8,7168]{3,2,0,1:T(8,128)(2,1)}, bf16[1,1,8,7168]{3,2,0,1:T(8,128)(2,1)S(1)}, u32[]{:S(2)}, u32[]{:S(2)}) %collective-permute-start.4) | collective-permute-done | bytes 114720 | tf_op jit(solution)/shard_map/ppermute | solution.py:58
  73.6 6.8 %collective-permute-done.5 = bf16[1,1,8,7168]{3,2,0,1:T(8,128)(2,1)S(1)} collective-permute-done((bf16[1,1,8,7168]{3,2,0,1:T(8,128)(2,1)}, bf16[1,1,8,7168]{3,2,0,1:T(8,128)(2,1)S(1)}, u32[]{:S(2)}, u32[]{:S(2)}) %collective-permute-start.5) | collective-permute-done | bytes 114720 | tf_op jit(solution)/shard_map/ppermute | solution.py:58
  80.4 7.8 %collective-permute-done.6 = bf16[1,1,8,7168]{3,2,0,1:T(8,128)(2,1)S(1)} collective-permute-done((bf16[1,1,8,7168]{3,2,0,1:T(8,128)(2,1)}, bf16[1,1,8,7168]{3,2,0,1:T(8,128)(2,1)S(1)}, u32[]{:S(2)}, u32[]{:S(2)}) %collective-permute-start.6) | collective-permute-done | bytes 114720 | tf_op jit(solution)/shard_map/ppermute | solution.py:58
  88.2 7.1 %collective-permute-done.7 = bf16[1,1,8,7168]{3,2,0,1:T(8,128)(2,1)S(1)} collective-permute-done((bf16[1,1,8,7168]{3,2,0,1:T(8,128)(2,1)S(1)}, bf16[1,1,8,7168]{3,2,0,1:T(8,128)(2,1)S(1)}, u32[]{:S(2)}, u32[]{:S(2)}) %collective-permute-start.7) | collective-permute-done | bytes 114720 | tf_op jit(solution)/shard_map/ppermute | solution.py:58
  95.4 6.6 %collective-permute-done.8 = bf16[1,1,8,7168]{3,2,0,1:T(8,128)(2,1)S(1)} collective-permute-done((bf16[1,1,8,7168]{3,2,0,1:T(8,128)(2,1)}, bf16[1,1,8,7168]{3,2,0,1:T(8,128)(2,1)S(1)}, u32[]{:S(2)}, u32[]{:S(2)}) %collective-permute-start.8) | collective-permute-done | bytes 114720 | tf_op jit(solution)/shard_map/ppermute | solution.py:58
  103.1 4.6 %collective-permute-done.9 = bf16[1,1,8,7168]{3,2,0,1:T(8,128)(2,1)S(1)} collective-permute-done((bf16[1,1,8,7168]{3,2,0,1:T(8,128)(2,1)S(1)}, bf16[1,1,8,7168]{3,2,0,1:T(8,128)(2,1)S(1)}, u32[]{:S(2)}, u32[]{:S(2)}) %collective-permute-start.9) | collective-permute-done | bytes 114720 | tf_op jit(solution)/shard_map/ppermute | solution.py:58
  107.8 3.6 %collective-permute-start.10 = (bf16[1,1,8,7168]{3,2,0,1:T(8,128)(2,1)S(1)}, bf16[1,1,8,7168]{3,2,0,1:T(8,128)(2,1)S(1)}, u32[]{:S(2)}, u32[]{:S(2)}) collective-permute-start(bf16[1,1,8,7168]{3,2,0,1:T(8,128)(2,1)S(1)} %get-tuple-element.9), channel_id=1, source_target_pairs={{0,22},{2,24},{4,26},{6,28},{8,30},{10,0},{12,2},{14,4},{16,6},{18... | collective-permute-start | bytes 344072 | tf_op jit(solution)/shard_map/ppermute | solution.py:58
  111.4 2.4 %collective-permute-done.10 = bf16[1,1,8,7168]{3,2,0,1:T(8,128)(2,1)S(1)} collective-permute-done((bf16[1,1,8,7168]{3,2,0,1:T(8,128)(2,1)S(1)}, bf16[1,1,8,7168]{3,2,0,1:T(8,128)(2,1)S(1)}, u32[]{:S(2)}, u32[]{:S(2)}) %collective-permute-start.10) | collective-permute-done | bytes 114720 | tf_op jit(solution)/shard_map/ppermute | solution.py:58
  113.9 4.4 %multiply_convert_fusion = bf16[128,512]{1,0:T(8,128)(2,1)S(1)} fusion(bf16[1,7168,512]{2,1,0:T(8,128)(2,1)} %param.8, bf16[16,1,8,7168]{3,2,0,1:T(8,128)(2,1)S(1)} %constant_dynamic-update-slice_fusion.14), kind=kOutput, calls=%fused_computation.16 | convolution fusion | flops 939851776 | bytes 9306112 | tf_op jit(solution)/shard_map/esd,edh->esh/dot_general | solution.py:66
  118.4 2.0 %all-gather = bf16[128,1024]{1,0:T(8,128)(2,1)S(1)} all-gather(bf16[128,512]{1,0:T(8,128)(2,1)S(1)} %multiply_convert_fusion), channel_id=2, replica_groups=mesh['expert'=16,'loop'=2] {'loop'}, dimensions={1}, use_global_device_ids=true | all-gather | bytes 393216 | tf_op jit(solution)/shard_map/all_gather | solution.py:71
  120.4 2.1 %fusion.7 = bf16[16,8,3584]{2,1,0:T(8,128)(2,1)} fusion(bf16[128,1024]{1,0:T(8,128)(2,1)S(1)} %all-gather, bf16[1,1024,3584]{2,1,0:T(8,128)(2,1)S(1)} %bitcast.33), kind=kOutput, calls=%fused_computation.7 | convolution fusion | flops 939982848 | bytes 8519680 | tf_op jit(solution)/shard_map/esh,ehd->esd/dot_general | solution.py:69
  122.4 9.3 %all-to-all-start = ((bf16[16,8,3584]{2,1,0:T(8,128)(2,1)}), bf16[16,8,3584]{2,1,0:T(8,128)(2,1)S(1)}, u32[]{:S(2)}, u32[]{:S(2)}) async-start(bf16[16,8,3584]{2,1,0:T(8,128)(2,1)} %fusion.7), calls=%async_computation | async-start | bytes 1835008 | tf_op jit(solution)/shard_map/all_to_all | solution.py:80
  132.0 22.0 %all-to-all-done = bf16[16,8,3584]{2,1,0:T(8,128)(2,1)S(1)} async-done(((bf16[16,8,3584]{2,1,0:T(8,128)(2,1)}), bf16[16,8,3584]{2,1,0:T(8,128)(2,1)S(1)}, u32[]{:S(2)}, u32[]{:S(2)}) %all-to-all-start) | async-done | bytes 917536 | tf_op jit(solution)/shard_map/all_to_all | solution.py:80
  154.0 3.6 %scatter_custom_fusion = f32[128,3584]{1,0:T(8,128)S(1)} fusion(s32[128]{0:T(128)S(1)} %reshape.121, bf16[16,8,3584]{2,1,0:T(8,128)(2,1)S(1)} %all-to-all-done, f32[128]{0:T(128)S(1)} %mul.30, f32[]{:T(128)} %constant.215.clone.1), kind=kCustom, calls=%fused_computation.9 | custom fusion | flops 1376256 | bytes 2753028 | tf_op jit(solution)/shard_map/scatter-add | solution.py:84
  (60 shorter events, 9.3 us)
Async XLA Ops:
  6.5 15.3 %all-gather.3.cloned.1.call-start = ((), (), s32[]{:S(2)}) async-start(), calls=%async_computation.1 | async-start | bytes 2752512 | tf_op jit(solution)/shard_map/all_gather | solution.py:47
  29.9 9.1 %collective-permute-start = (bf16[1,1,8,7168]{3,2,0,1:T(8,128)(2,1)S(1)}, bf16[1,1,8,7168]{3,2,0,1:T(8,128)(2,1)S(1)}, u32[]{:S(2)}, u32[]{:S(2)}) collective-permute-start(bf16[1,1,8,7168]{3,2,0,1:T(8,128)(2,1)S(1)} %constant_dynamic-slice_fusion.14), channel_id=1, source_target_pairs={{0,2},{2,4},{4,6},{6,8},{8,10},{10,12},{12,14},{14,16},{16,18},{18... | collective-permute-start | bytes 344072 | tf_op jit(solution)/shard_map/ppermute | solution.py:58
  39.8 9.2 %collective-permute-start.1 = (bf16[1,1,8,7168]{3,2,0,1:T(8,128)(2,1)S(1)}, bf16[1,1,8,7168]{3,2,0,1:T(8,128)(2,1)S(1)}, u32[]{:S(2)}, u32[]{:S(2)}) collective-permute-start(bf16[1,1,8,7168]{3,2,0,1:T(8,128)(2,1)S(1)} %get-tuple-element.18), channel_id=1, source_target_pairs={{0,4},{2,6},{4,8},{6,10},{8,12},{10,14},{12,16},{14,18},{16,20},{1... | collective-permute-start | bytes 344072 | tf_op jit(solution)/shard_map/ppermute | solution.py:58
  39.8 74.1 %collective-permute-start.14 = (bf16[1,1,8,7168]{3,2,0,1:T(8,128)(2,1)S(1)}, bf16[1,1,8,7168]{3,2,0,1:T(8,128)(2,1)S(1)}, u32[]{:S(2)}, u32[]{:S(2)}) collective-permute-start(bf16[1,1,8,7168]{3,2,0,1:T(8,128)(2,1)S(1)} %get-tuple-element.5), channel_id=1, source_target_pairs={{0,30},{2,0},{4,2},{6,4},{8,6},{10,8},{12,10},{14,12},{16,14},{18,... | collective-permute-start | bytes 344072 | tf_op jit(solution)/shard_map/ppermute | solution.py:58
  42.1 71.8 %collective-permute-start.13 = (bf16[1,1,8,7168]{3,2,0,1:T(8,128)(2,1)S(1)}, bf16[1,1,8,7168]{3,2,0,1:T(8,128)(2,1)S(1)}, u32[]{:S(2)}, u32[]{:S(2)}) collective-permute-start(bf16[1,1,8,7168]{3,2,0,1:T(8,128)(2,1)S(1)} %get-tuple-element.6), channel_id=1, source_target_pairs={{0,28},{2,30},{4,0},{6,2},{8,4},{10,6},{12,8},{14,10},{16,12},{18,... | collective-permute-start | bytes 344072 | tf_op jit(solution)/shard_map/ppermute | solution.py:58
  44.6 69.3 %collective-permute-start.12 = (bf16[1,1,8,7168]{3,2,0,1:T(8,128)(2,1)S(1)}, bf16[1,1,8,7168]{3,2,0,1:T(8,128)(2,1)S(1)}, u32[]{:S(2)}, u32[]{:S(2)}) collective-permute-start(bf16[1,1,8,7168]{3,2,0,1:T(8,128)(2,1)S(1)} %get-tuple-element.7), channel_id=1, source_target_pairs={{0,26},{2,28},{4,30},{6,0},{8,2},{10,4},{12,6},{14,8},{16,10},{18,... | collective-permute-start | bytes 344072 | tf_op jit(solution)/shard_map/ppermute | solution.py:58
  45.9 67.8 %collective-permute-start.11 = (bf16[1,1,8,7168]{3,2,0,1:T(8,128)(2,1)S(1)}, bf16[1,1,8,7168]{3,2,0,1:T(8,128)(2,1)S(1)}, u32[]{:S(2)}, u32[]{:S(2)}) collective-permute-start(bf16[1,1,8,7168]{3,2,0,1:T(8,128)(2,1)S(1)} %get-tuple-element.8), channel_id=1, source_target_pairs={{0,24},{2,26},{4,28},{6,30},{8,0},{10,2},{12,4},{14,6},{16,8},{18,... | collective-permute-start | bytes 344072 | tf_op jit(solution)/shard_map/ppermute | solution.py:58
  49.1 7.5 %collective-permute-start.2 = (bf16[1,1,8,7168]{3,2,0,1:T(8,128)(2,1)S(1)}, bf16[1,1,8,7168]{3,2,0,1:T(8,128)(2,1)S(1)}, u32[]{:S(2)}, u32[]{:S(2)}) collective-permute-start(bf16[1,1,8,7168]{3,2,0,1:T(8,128)(2,1)S(1)} %get-tuple-element.17), channel_id=1, source_target_pairs={{0,6},{2,8},{4,10},{6,12},{8,14},{10,16},{12,18},{14,20},{16,22},{... | collective-permute-start | bytes 344072 | tf_op jit(solution)/shard_map/ppermute | solution.py:58
  56.6 6.8 %collective-permute-start.3 = (bf16[1,1,8,7168]{3,2,0,1:T(8,128)(2,1)}, bf16[1,1,8,7168]{3,2,0,1:T(8,128)(2,1)S(1)}, u32[]{:S(2)}, u32[]{:S(2)}) collective-permute-start(bf16[1,1,8,7168]{3,2,0,1:T(8,128)(2,1)} %get-tuple-element.16), channel_id=1, source_target_pairs={{0,8},{2,10},{4,12},{6,14},{8,16},{10,18},{12,20},{14,22},{16,24},... | collective-permute-start | bytes 344072 | tf_op jit(solution)/shard_map/ppermute | solution.py:58
  63.4 10.2 %collective-permute-start.4 = (bf16[1,1,8,7168]{3,2,0,1:T(8,128)(2,1)}, bf16[1,1,8,7168]{3,2,0,1:T(8,128)(2,1)S(1)}, u32[]{:S(2)}, u32[]{:S(2)}) collective-permute-start(bf16[1,1,8,7168]{3,2,0,1:T(8,128)(2,1)} %get-tuple-element.15), channel_id=1, source_target_pairs={{0,10},{2,12},{4,14},{6,16},{8,18},{10,20},{12,22},{14,24},{16,26}... | collective-permute-start | bytes 344072 | tf_op jit(solution)/shard_map/ppermute | solution.py:58
  73.6 6.8 %collective-permute-start.5 = (bf16[1,1,8,7168]{3,2,0,1:T(8,128)(2,1)}, bf16[1,1,8,7168]{3,2,0,1:T(8,128)(2,1)S(1)}, u32[]{:S(2)}, u32[]{:S(2)}) collective-permute-start(bf16[1,1,8,7168]{3,2,0,1:T(8,128)(2,1)} %get-tuple-element.14), channel_id=1, source_target_pairs={{0,12},{2,14},{4,16},{6,18},{8,20},{10,22},{12,24},{14,26},{16,28}... | collective-permute-start | bytes 344072 | tf_op jit(solution)/shard_map/ppermute | solution.py:58
  80.4 7.8 %collective-permute-start.6 = (bf16[1,1,8,7168]{3,2,0,1:T(8,128)(2,1)}, bf16[1,1,8,7168]{3,2,0,1:T(8,128)(2,1)S(1)}, u32[]{:S(2)}, u32[]{:S(2)}) collective-permute-start(bf16[1,1,8,7168]{3,2,0,1:T(8,128)(2,1)} %get-tuple-element.13), channel_id=1, source_target_pairs={{0,14},{2,16},{4,18},{6,20},{8,22},{10,24},{12,26},{14,28},{16,30}... | collective-permute-start | bytes 344072 | tf_op jit(solution)/shard_map/ppermute | solution.py:58
  88.2 7.1 %collective-permute-start.7 = (bf16[1,1,8,7168]{3,2,0,1:T(8,128)(2,1)S(1)}, bf16[1,1,8,7168]{3,2,0,1:T(8,128)(2,1)S(1)}, u32[]{:S(2)}, u32[]{:S(2)}) collective-permute-start(bf16[1,1,8,7168]{3,2,0,1:T(8,128)(2,1)S(1)} %get-tuple-element.12), channel_id=1, source_target_pairs={{0,16},{2,18},{4,20},{6,22},{8,24},{10,26},{12,28},{14,30},{16,0},... | collective-permute-start | bytes 344072 | tf_op jit(solution)/shard_map/ppermute | solution.py:58
  95.3 6.8 %collective-permute-start.8 = (bf16[1,1,8,7168]{3,2,0,1:T(8,128)(2,1)}, bf16[1,1,8,7168]{3,2,0,1:T(8,128)(2,1)S(1)}, u32[]{:S(2)}, u32[]{:S(2)}) collective-permute-start(bf16[1,1,8,7168]{3,2,0,1:T(8,128)(2,1)} %get-tuple-element.11), channel_id=1, source_target_pairs={{0,18},{2,20},{4,22},{6,24},{8,26},{10,28},{12,30},{14,0},{16,2},{... | collective-permute-start | bytes 344072 | tf_op jit(solution)/shard_map/ppermute | solution.py:58
  102.1 5.7 %collective-permute-start.9 = (bf16[1,1,8,7168]{3,2,0,1:T(8,128)(2,1)S(1)}, bf16[1,1,8,7168]{3,2,0,1:T(8,128)(2,1)S(1)}, u32[]{:S(2)}, u32[]{:S(2)}) collective-permute-start(bf16[1,1,8,7168]{3,2,0,1:T(8,128)(2,1)S(1)} %get-tuple-element.10), channel_id=1, source_target_pairs={{0,20},{2,22},{4,24},{6,26},{8,28},{10,30},{12,0},{14,2},{16,4},{1... | collective-permute-start | bytes 344072 | tf_op jit(solution)/shard_map/ppermute | solution.py:58
  107.8 6.0 %collective-permute-start.10 = (bf16[1,1,8,7168]{3,2,0,1:T(8,128)(2,1)S(1)}, bf16[1,1,8,7168]{3,2,0,1:T(8,128)(2,1)S(1)}, u32[]{:S(2)}, u32[]{:S(2)}) collective-permute-start(bf16[1,1,8,7168]{3,2,0,1:T(8,128)(2,1)S(1)} %get-tuple-element.9), channel_id=1, source_target_pairs={{0,22},{2,24},{4,26},{6,28},{8,30},{10,0},{12,2},{14,4},{16,6},{18... | collective-permute-start | bytes 344072 | tf_op jit(solution)/shard_map/ppermute | solution.py:58
  113.8 6.5 %slice-start = ((s8[7340032]{0:T(1024)(128)(4,1)}), s8[4194304]{0:T(1024)(128)(4,1)S(1)}, s32[]{:S(2)}) async-start(s8[7340032]{0:T(1024)(128)(4,1)} %bitcast.32), calls=%async_computation.2 | async-start | bytes 8388608
  113.9 6.4 %slice-start.1 = ((s8[7340032]{0:T(1024)(128)(4,1)}), s8[3145728]{0:T(1024)(128)(4,1)S(1)}, s32[]{:S(2)}) async-start(s8[7340032]{0:T(1024)(128)(4,1)} %bitcast.32), calls=%async_computation.3 | async-start | bytes 6291456
  122.4 9.4 %copy-start = (s32[128,8]{0,1:T(8,128)S(1)}, s32[128,8]{0,1:T(8,128)}, u32[]{:S(2)}) copy-start(s32[128,8]{0,1:T(8,128)} %param.6) | copy-start | bytes 12292
  122.4 9.4 %copy-start.1 = (f32[128,8]{0,1:T(8,128)S(1)}, f32[128,8]{0,1:T(8,128)}, u32[]{:S(2)}) copy-start(f32[128,8]{0,1:T(8,128)} %param.7) | copy-start | bytes 12292
  122.4 31.6 %all-to-all-start = ((bf16[16,8,3584]{2,1,0:T(8,128)(2,1)}), bf16[16,8,3584]{2,1,0:T(8,128)(2,1)S(1)}, u32[]{:S(2)}, u32[]{:S(2)}) async-start(bf16[16,8,3584]{2,1,0:T(8,128)(2,1)} %fusion.7), calls=%async_computation | async-start | bytes 1835008 | tf_op jit(solution)/shard_map/all_to_all | solution.py:80
Sparse Core Ops, SparseCore 0:
  8.9 12.8 all-gather.2
